TPU v7x, 32 devices: a whole 2x2x4 slice. The times are simulated.
32 devices in a mesh: groups: 2 (over x), tile: 16 (over z, y, core).
Axes of the slice: x: 2, y: 2, z: 4, core: 2. Of those that a mesh axis runs over, the one named last changes fastest.
Arguments:
- probes: float32 [8, 262144], P(None, ('groups', 'tile')), parts along dimension 1, may hold values from -6 to 6
- level_set: float32 [262144], P(('groups', 'tile')), parts along dimension 0, may hold values from -6 to 6
- unit_label: int32 [262144], P(('groups', 'tile')), parts along dimension 0, may hold values from 0 to 3
- contrast: float32 [8], P('groups'), parts along dimension 0, may hold values from 0.2 to 1.5
- station_weight: float32 [65536], P('groups'), parts along dimension 0, may hold values from 0.2 to 2
- u_factor: bfloat16 [4096, 32, 512], P(('groups', 'tile')), parts along dimension 0, may hold values from -1 to 1
- v_factor: bfloat16 [4096, 32, 512], P(('groups', 'tile')), parts along dimension 0, may hold values from -0.25 to 0.25
- col_owner: int32 [4096, 1], P('groups'), parts along dimension 0, may hold values from 0 to 15; in each aligned block of 128 rows (0 to 127, 128 to 255, ...) at most 16 rows name the same one
- col_local: int32 [4096], P('groups'), parts along dimension 0, may hold values from 0 to 15
- row_owner: int32 [4096, 1], P('groups'), parts along dimension 0, may hold values from 0 to 15; in each aligned block of 128 rows (0 to 127, 128 to 255, ...) at most 16 rows name the same one
- row_local: int32 [4096], P('groups'), parts along dimension 0, may hold values from 0 to 3
- tile_rank: int32 [4096], P('groups'), parts along dimension 0, may hold values from 8 to 32
Outputs:
- hessian_probes: float32 [8, 262144], P(None, ('groups', 'tile')), parts along dimension 1
There are 2 independent parts, one for each index of `groups`. A program takes and returns all parts, laid end to end along the dimension named above; each array names one. Nothing has to cross between parts.
Inputs may be any that keep to these rules, and one draw needn't show every extreme that they name: `col_owner`: among the 128 tiles of one device (aligned blocks of 128 entries) no owner is named more than 16 times, a bound that some block reaches. `row_owner`: among the 128 tiles of one device (aligned blocks of 128 entries) no owner is named more than 16 times, a bound that some block reaches.
All inputs are finite; a program needn't handle non-finite values.
Results may differ from a plain program's by a relative error of at most 0.005.
Values may be sent and summed in bfloat16 or wider, within the bound.
No kernel may reach another device: no remote copies, remote signals or barrier semaphores. Data moves between devices by JAX's collectives and lax.ppermute only.
A program may use at most 64 MiB of HBM per device.

v0:
```python
import jax
import jax.numpy as jnp
from jax import lax
from jax.sharding import PartitionSpec as P

HIGHEST = lax.Precision.HIGHEST


def rank_within(owner_table, target, capacity):
    matches = (owner_table == target).astype(jnp.int32)
    position = jnp.cumsum(matches, axis=-1) - 1
    slot_ids = jnp.arange(capacity, dtype=jnp.int32)
    chosen = (matches[:, None, :] == 1) & (position[:, None, :] == slot_ids[None, :, None])
    return chosen.astype(jnp.float32)


def sender_table(owner_table, local_table, target, capacity, block_count):
    chosen = rank_within(owner_table, target, capacity)
    local_match = (
        local_table[:, :, None] == jnp.arange(block_count, dtype=jnp.int32)[None, None, :]
    ).astype(jnp.float32)
    return jnp.einsum(
        "pqs,psb->pqb", chosen, local_match, precision=HIGHEST, preferred_element_type=jnp.float32
    )


def receiver_table(owner_mine, capacity, peer_count):
    count = owner_mine.shape[0]
    positions = jnp.arange(count, dtype=jnp.int32)
    earlier = (owner_mine[None, :] == owner_mine[:, None]) & (
        positions[None, :] < positions[:, None]
    )
    order = jnp.sum(earlier.astype(jnp.int32), axis=1)
    target = owner_mine * capacity + order
    return (target[:, None] == jnp.arange(peer_count * capacity, dtype=jnp.int32)[None, :]).astype(
        jnp.float32
    )


def shards(
    probes,
    level_set,
    unit_label,
    contrast,
    station_weight,
    u_factor,
    v_factor,
    col_owner,
    col_local,
    row_owner,
    row_local,
    tile_rank,
):
    peer_count = lax.axis_size("tile")
    own_index = lax.axis_index("tile")
    tile_count, rank_max, station_width = u_factor.shape
    cell_width = v_factor.shape[2]
    probe_count, cell_total = probes.shape
    cell_blocks = cell_total // cell_width
    station_blocks = station_weight.shape[0] // (peer_count * station_width)
    capacity = max(2, 2 * tile_count // peer_count)
    flat_cells = probe_count * cell_width
    flat_stations = probe_count * station_width
    col_owner_all = col_owner.reshape(peer_count, tile_count)
    col_local_all = col_local.reshape(peer_count, tile_count)
    row_owner_all = row_owner.reshape(peer_count, tile_count)
    row_local_all = row_local.reshape(peer_count, tile_count)
    col_owner_mine = lax.dynamic_index_in_dim(col_owner_all, own_index, 0, keepdims=False)
    col_local_mine = lax.dynamic_index_in_dim(col_local_all, own_index, 0, keepdims=False)
    row_owner_mine = lax.dynamic_index_in_dim(row_owner_all, own_index, 0, keepdims=False)
    row_local_mine = lax.dynamic_index_in_dim(row_local_all, own_index, 0, keepdims=False)
    rank_mine = lax.dynamic_index_in_dim(
        tile_rank.reshape(peer_count, tile_count), own_index, 0, keepdims=False
    )
    unit_count = contrast.shape[0]
    unit_match = (unit_label[None, :] == jnp.arange(unit_count, dtype=jnp.int32)[:, None]).astype(
        jnp.float32
    )
    scaling = jnp.sum(unit_match * contrast[:, None], axis=0) / (1.0 + level_set * level_set)
    scaled = (probes * scaling[None, :]).astype(jnp.bfloat16)
    cell_rows = (
        scaled.reshape(probe_count, cell_blocks, cell_width)
        .transpose(1, 0, 2)
        .reshape(cell_blocks, flat_cells)
    )
    col_global = col_owner_mine * cell_blocks + col_local_mine
    col_slots = receiver_table(col_owner_mine, capacity, peer_count)
    col_choice = sender_table(col_owner_all, col_local_all, own_index, capacity, cell_blocks)
    piece = lax.all_gather(cell_rows, "tile", axis=0, tiled=True)
    rows_here = piece.shape[0]
    match = (col_global[:, None] == jnp.arange(rows_here, dtype=jnp.int32)[None, :]).astype(
        jnp.bfloat16
    )
    fetched = jnp.dot(match, piece, preferred_element_type=jnp.float32)
    tile_cells = fetched.astype(jnp.bfloat16).reshape(tile_count, probe_count, cell_width)
    keep = (jnp.arange(rank_max, dtype=jnp.int32)[None, :] < rank_mine[:, None]).astype(
        jnp.float32
    )[:, None, :]
    coeff = jnp.einsum("tkc,trc->tkr", tile_cells, v_factor, preferred_element_type=jnp.float32)
    coeff = (coeff * keep).astype(jnp.bfloat16)
    partial_value = jnp.einsum(
        "tkr,trs->tks", coeff, u_factor, preferred_element_type=jnp.float32
    ).reshape(tile_count, flat_stations)
    row_global = row_owner_mine * station_blocks + row_local_mine
    match = (
        jnp.arange(station_blocks * lax.axis_size("tile"), dtype=jnp.int32)[:, None]
        == row_global[None, :]
    ).astype(jnp.float32)
    predicted = lax.psum_scatter(
        jnp.dot(match, partial_value, precision=HIGHEST, preferred_element_type=jnp.float32),
        "tile",
        scatter_dimension=0,
        tiled=True,
    )
    weight_mine = lax.dynamic_slice_in_dim(
        station_weight, own_index * station_blocks * station_width, station_blocks * station_width
    )
    weighted = (
        predicted.reshape(station_blocks, probe_count, station_width)
        * weight_mine.reshape(station_blocks, 1, station_width)
    ).astype(jnp.bfloat16)
    weighted = weighted.reshape(station_blocks, flat_stations)
    row_choice = sender_table(row_owner_all, row_local_all, own_index, capacity, station_blocks)
    outgoing_data = jnp.einsum(
        "pqb,bf->pqf", row_choice.astype(jnp.bfloat16), weighted, preferred_element_type=jnp.float32
    ).astype(jnp.bfloat16)
    incoming_data = lax.all_to_all(outgoing_data, "tile", split_axis=0, concat_axis=0, tiled=True)
    row_slots = receiver_table(row_owner_mine, capacity, peer_count)
    tile_data = jnp.dot(
        row_slots.astype(jnp.bfloat16),
        incoming_data.reshape(peer_count * capacity, flat_stations),
        preferred_element_type=jnp.float32,
    )
    tile_weighted = tile_data.astype(jnp.bfloat16).reshape(tile_count, probe_count, station_width)
    back = jnp.einsum("tks,trs->tkr", tile_weighted, u_factor, preferred_element_type=jnp.float32)
    back = (back * keep).astype(jnp.bfloat16)
    spread = jnp.einsum("tkr,trc->tkc", back, v_factor, preferred_element_type=jnp.float32).reshape(
        tile_count, flat_cells
    )
    slot_rows = col_slots.T.reshape(peer_count, capacity, tile_count)
    returned = jnp.einsum(
        "pqt,tf->pqf", slot_rows, spread, precision=HIGHEST, preferred_element_type=jnp.float32
    )
    arrived = lax.all_to_all(returned, "tile", split_axis=0, concat_axis=0, tiled=True)
    summed = jnp.einsum(
        "pqb,pqf->bf", col_choice, arrived, precision=HIGHEST, preferred_element_type=jnp.float32
    )
    gradient = (
        summed.reshape(cell_blocks, probe_count, cell_width)
        .transpose(1, 0, 2)
        .reshape(probe_count, cell_total)
    )
    return scaling[None, :] * gradient


def solution(mesh):
    placed = (
        P(None, ("groups", "tile")),
        P(("groups", "tile")),
        P(("groups", "tile")),
        P("groups"),
        P("groups"),
        P(("groups", "tile"), None, None),
        P(("groups", "tile"), None, None),
        P("groups", None),
        P("groups"),
        P("groups", None),
        P("groups"),
        P("groups"),
    )
    return jax.shard_map(
        shards, mesh=mesh, in_specs=placed, out_specs=P(None, ("groups", "tile")), check_vma=False
    )
```

profile of v0, /device:TPU:13, one launch (start us, length us, event | category | flops | bytes accessed | tf_op | source)
XLA Modules:
  0.0 335.7 jit_solution(17233125049416313303)
XLA Ops:
  6.5 0.0 all-gather.2.cloned.1.call-start
  6.5 0.9 select_reduce_fusion
  7.5 0.8 add_divide_fusion
  8.2 1.0 multiply_convert_fusion
  9.2 0.7 copy.15
  9.9 0.0 all-gather.2.cloned.1.call-update
  10.0 0.0 all-reduce.3.cloned.1.call-start
  10.0 0.7 dynamic_slice.24
  10.7 0.7 fusion.35
  11.4 0.7 fusion.38
  12.2 0.1 fusion.23
  12.3 38.9 %all-gather.2.cloned.1.call-done = bf16[256,4096]{1,0:T(8,128)(2,1)} async-done(((bf16[16,4096]{1,0:T(8,128)(2,1)}), bf16[256,4096]{1,0:T(8,128)(2,1)}) %all-gather.2.cloned.1.call-update) | async-done | bytes 2097168 | tf_op jit(solution)/shard_map/all_gather | solution.py:89
  51.2 2.1 convolution_convert_fusion.2
  53.2 0.4 copy.16
  53.6 5.2 %fusion.3 = f32[128,8,512]{2,1,0:T(8,128)S(1)} fusion(bf16[128,32,512]{2,1,0:T(8,128)(2,1)} %param.17, bf16[128,8,512]{2,1,0:T(8,128)(2,1)S(1)} %bitcast.63, bf16[128,32,512]{2,1,0:T(8,128)(2,1)} %param.18, f32[128,32]{1,0:T(8,128)S(1)} %fusion.23), kind=kOutput, calls=%fused_computation.8 | convolution fusion | flops 67174400 | bytes 11550720 | tf_op jit(solution)/shard_map/tkr,trs->tks/dot_general | solution.py:101
  58.8 1.6 copy.17
  60.5 0.0 copy-start.1
  60.5 0.0 copy-start.2
  60.5 0.0 copy-start.4
  60.5 0.0 copy-start.3
  60.5 1.9 fusion.28
  62.4 0.0 all-reduce.3.cloned.1.call-update
  62.5 0.0 copy-done.1
  62.5 0.0 copy-done.2
  62.5 0.3 reduce_window_sum.18
  62.8 0.0 copy-done.4
  62.8 0.6 dynamic-slice
  64.1 0.0 copy-done.3
  64.1 0.2 convolution_convert_fusion.3
  64.3 89.8 %all-reduce.3.cloned.1.call-done = f32[64,4096]{1,0:T(8,128)} async-done(((f32[64,4096]{1,0:T(8,128)}), f32[64,4096]{1,0:T(8,128)}) %all-reduce.3.cloned.1.call-update) | async-done | bytes 1048592
  154.0 3.1 convolution_convert_fusion
  157.1 6.8 %all-to-all-start = ((bf16[16,16,4096]{2,1,0:T(8,128)(2,1)}), bf16[16,16,4096]{2,1,0:T(8,128)(2,1)S(1)}, u32[]{:S(2)}, u32[]{:S(2)}) async-start(bf16[16,16,4096]{2,1,0:T(8,128)(2,1)} %convolution_convert_fusion), calls=%async_computation | async-start | bytes 4194304 | tf_op jit(solution)/shard_map/all_to_all | solution.py:127
  163.9 0.2 convert_reduce_fusion
  164.0 0.2 convert_reduce_fusion.1
  164.3 47.0 %all-to-all-done = bf16[16,16,4096]{2,1,0:T(8,128)(2,1)S(1)} async-done(((bf16[16,16,4096]{2,1,0:T(8,128)(2,1)}), bf16[16,16,4096]{2,1,0:T(8,128)(2,1)S(1)}, u32[]{:S(2)}, u32[]{:S(2)}) %all-to-all-start) | async-done | bytes 2097184 | tf_op jit(solution)/shard_map/all_to_all | solution.py:127
  211.3 0.5 convolution_convert_fusion.1
  211.8 0.4 copy.19
  212.2 6.5 %fusion.2 = f32[128,8,512]{2,1,0:T(8,128)} fusion(bf16[128,32,512]{2,1,0:T(8,128)(2,1)} %param.18, bf16[128,8,512]{2,1,0:T(8,128)(2,1)S(1)} %bitcast.62, bf16[128,32,512]{2,1,0:T(8,128)(2,1)} %param.17, f32[128,32]{1,0:T(8,128)S(1)} %fusion.23), kind=kOutput, calls=%fused_computation.7 | convolution fusion | flops 67174400 | bytes 11550720 | tf_op jit(solution)/shard_map/tkr,trc->tkc/dot_general | solution.py:137
  218.7 1.7 reshape.169
  220.5 3.8 %fusion.11 = f32[16,16,4096]{2,1,0:T(8,128)} fusion(f32[128,4096,1]{1,0,2:T(8,128)S(1)} %reshape.169, s32[16,16]{1,0:T(8,128)S(1)} %multiply_add_fusion, s32[128]{0:T(128)S(1)} %multiply_add_fusion.2), kind=kOutput, calls=%fused_computation.25 | convolution fusion | flops 1610645504 | bytes 6292992 | tf_op jit(solution)/shard_map/pqt,tf->pqf/dot_general | solution.py:141
  224.3 5.0 %all-to-all-start.1 = ((f32[16,16,4096]{2,1,0:T(8,128)}), f32[16,16,4096]{2,1,0:T(8,128)}, u32[]{:S(2)}, u32[]{:S(2)}) async-start(f32[16,16,4096]{2,1,0:T(8,128)} %fusion.11), calls=%async_computation.1 | async-start | bytes 8388608 | tf_op jit(solution)/shard_map/all_to_all | solution.py:144
  229.4 0.3 reduce_window_sum.17
  229.7 0.0 copy-done
  229.7 0.2 fusion.7
  229.8 92.0 %all-to-all-done.1 = f32[16,16,4096]{2,1,0:T(8,128)} async-done(((f32[16,16,4096]{2,1,0:T(8,128)}), f32[16,16,4096]{2,1,0:T(8,128)}, u32[]{:S(2)}, u32[]{:S(2)}) %all-to-all-start.1) | async-done | bytes 4194336 | tf_op jit(solution)/shard_map/all_to_all | solution.py:144
  321.8 6.2 %fusion.40 = f32[16,4096,1]{1,0,2:T(8,128)S(1)} fusion(f32[16,16,16]{1,2,0:T(8,128)S(1)} %fusion.7, f32[16,16,4096]{2,1,0:T(8,128)} %all-to-all-done.1), kind=kOutput, calls=%fused_computation.75 | convolution fusion | flops 201326592 | bytes 4472832 | tf_op jit(solution)/shard_map/pqb,pqf->bf/dot_general | solution.py:145
  328.0 0.2 copy.20
  328.2 0.7 broadcast_multiply_fusion
  (10 shorter events, 0.1 us)
Async XLA Ops:
  6.5 44.6 %all-gather.2.cloned.1.call-start = ((), (), s32[]{:S(2)}) async-start(), calls=%async_computation.2 | async-start | bytes 2228224 | tf_op jit(solution)/shard_map/all_gather | solution.py:89
  10.0 144.1 %all-reduce.3.cloned.1.call-start = ((), (), s32[]{:S(2)}) async-start(), calls=%async_computation.3 | async-start | bytes 2097152
  60.5 2.0 copy-start.1
  60.5 2.0 copy-start.2
  60.5 2.3 copy-start.4
  60.5 3.6 %copy-start.3 = (s32[2048]{0:T(1024)S(1)}, s32[2048]{0:T(1024)}, u32[]{:S(2)}) copy-start(s32[2048]{0:T(1024)} %param.22) | copy-start | bytes 24580
  157.1 54.2 %all-to-all-start = ((bf16[16,16,4096]{2,1,0:T(8,128)(2,1)}), bf16[16,16,4096]{2,1,0:T(8,128)(2,1)S(1)}, u32[]{:S(2)}, u32[]{:S(2)}) async-start(bf16[16,16,4096]{2,1,0:T(8,128)(2,1)} %convolution_convert_fusion), calls=%async_computation | async-start | bytes 4194304 | tf_op jit(solution)/shard_map/all_to_all | solution.py:127
  224.3 5.3 %copy-start = (s32[2048]{0:T(1024)S(1)}, s32[2048]{0:T(1024)}, u32[]{:S(2)}) copy-start(s32[2048]{0:T(1024)} %param.20) | copy-start | bytes 24580
  224.3 97.5 %all-to-all-start.1 = ((f32[16,16,4096]{2,1,0:T(8,128)}), f32[16,16,4096]{2,1,0:T(8,128)}, u32[]{:S(2)}, u32[]{:S(2)}) async-start(f32[16,16,4096]{2,1,0:T(8,128)} %fusion.11), calls=%async_computation.1 | async-start | bytes 8388608 | tf_op jit(solution)/shard_map/all_to_all | solution.py:144
Sparse Core Ops, SparseCore 0:
  10.1 41.0 all-gather.1
  62.6 91.4 all-reduce.2
where the time goes:
time: 336 us
  waiting for transfers between devices  268 us (80%)
  matrix products  29.6 us (9%)
  between operations  14.3 us (4%)
  starting transfers between devices  11.8 us (4%)
  local copies, waits for them, and re-layouts  6.41 us (2%)
  other arithmetic  5.89 us (2%)
    all_to_all x1, waiting for transfers between devices, shards(): lax.all_to_all(returned, 'tile', split_axis=0, concat_axis=0, tiled=True)  92 us
    unnamed x3, waiting for transfers between devices  89.8 us
    all_to_all x1, waiting for transfers between devices, shards(): lax.all_to_all(outgoing_data, 'tile', split_axis=0, concat_axis=0, tiled=...  47 us
    all_gather x1, waiting for transfers between devices, shards(): piece = lax.all_gather(cell_rows, 'tile', axis=0, tiled=True)  38.9 us
    all_to_all x1, starting transfers between devices, shards(): lax.all_to_all(outgoing_data, 'tile', split_axis=0, concat_axis=0, tiled=...  6.76 us
  transfers between devices with their start and end apart: 4, of which 4 were waited for; matrix products, arithmetic and copies ran while one was open for 1% of the time, Pallas kernels for 0%

commit v1 on v0

--- a/solution.py
+++ b/solution.py
@@ -86,7 +86,12 @@
     col_global = col_owner_mine * cell_blocks + col_local_mine
     col_slots = receiver_table(col_owner_mine, capacity, peer_count)
     col_choice = sender_table(col_owner_all, col_local_all, own_index, capacity, cell_blocks)
-    piece = lax.all_gather(cell_rows, "tile", axis=0, tiled=True)
+    ring = [cell_rows]
+    for hop in range(15):
+        ring.append(lax.ppermute(ring[-1], "tile", [(dev, (dev + 1) % 16) for dev in range(16)]))
+    piece = jnp.roll(
+        jnp.concatenate(ring[::-1], axis=0), (lax.axis_index("tile") + 1) * ring[0].shape[0], axis=0
+    )
     rows_here = piece.shape[0]
     match = (col_global[:, None] == jnp.arange(rows_here, dtype=jnp.int32)[None, :]).astype(
         jnp.bfloat16

time: 336 us -> 397 us (1.18)
  starting transfers between devices: 11.8 us -> 60.5 us
  waiting for transfers between devices: 268 us -> 281 us
    ppermute x0 -> x15, starting transfers between devices: none -> 48.7 us  [shards(): lax.ppermute(ring[-1], 'tile', [(dev, (dev + 1) % 16) for dev in range(16)])]
    all_gather x1 -> x0, waiting for transfers between devices: 38.9 us -> none  [shards(): piece = lax.all_gather(cell_rows, 'tile', axis=0, tiled=True)]
    ppermute x0 -> x15, waiting for transfers between devices: none -> 27 us  [shards(): lax.ppermute(ring[-1], 'tile', [(dev, (dev + 1) % 16) for dev in range(16)])]
    unnamed x3 -> x2, waiting for transfers between devices: 89.8 us -> 115 us
  transfers between devices with their start and end apart: 4 -> 18, of which waited for: 4 -> 18; matrix products, arithmetic and copies ran while one was open for 1% -> 1% of each run, Pallas kernels for 0% -> 0%
where the time goes in v1:
time: 397 us; the launch traced here: 396 us
  waiting for transfers between devices  281 us (71%)
  starting transfers between devices  60.5 us (15%)
  matrix products  28 us (7%)
  between operations  14.5 us (4%)
  local copies, waits for them, and re-layouts  6.1 us (2%)
  other arithmetic  5.89 us (1%)
    unnamed x2, waiting for transfers between devices  115 us
    all_to_all x1, waiting for transfers between devices, shards(): lax.all_to_all(returned, 'tile', split_axis=0, concat_axis=0, tiled=True)  92 us
    ppermute x15, starting transfers between devices, shards(): lax.ppermute(ring[-1], 'tile', [(dev, (dev + 1) % 16) for dev in range(16)])  48.7 us
    all_to_all x1, waiting for transfers between devices, shards(): lax.all_to_all(outgoing_data, 'tile', split_axis=0, concat_axis=0, tiled=...  47 us
    ppermute x15, waiting for transfers between devices, shards(): lax.ppermute(ring[-1], 'tile', [(dev, (dev + 1) % 16) for dev in range(16)])  27 us
  transfers between devices with their start and end apart: 18, of which 18 were waited for; matrix products, arithmetic and copies ran while one was open for 1% of the time, Pallas kernels for 0%

profile of v1, /device:TPU:13, one launch (start us, length us, event | category | flops | bytes accessed | tf_op | source)
XLA Modules:
  0.0 396.1 jit_solution(16826541345054870398)
XLA Ops:
  6.5 0.9 select_reduce_fusion
  7.5 0.8 add_divide_fusion
  8.2 1.0 multiply_convert_fusion
  9.3 1.9 collective-permute-start
  11.1 1.9 collective-permute-done
  13.1 3.3 collective-permute-start.1
  16.4 1.9 collective-permute-done.1
  18.4 3.3 collective-permute-start.2
  21.7 1.9 collective-permute-done.2
  23.7 3.3 collective-permute-start.3
  27.0 1.9 collective-permute-done.3
  29.0 3.3 collective-permute-start.4
  32.3 1.9 collective-permute-done.4
  34.3 3.3 collective-permute-start.5
  37.6 1.9 collective-permute-done.5
  39.5 3.3 collective-permute-start.6
  42.9 1.9 collective-permute-done.6
  44.8 3.3 collective-permute-start.7
  48.2 1.9 collective-permute-done.7
  50.1 3.3 collective-permute-start.8
  53.5 1.9 collective-permute-done.8
  55.4 3.3 collective-permute-start.9
  58.8 1.9 collective-permute-done.9
  60.7 3.3 collective-permute-start.10
  64.1 1.9 collective-permute-done.10
  66.0 3.3 collective-permute-start.11
  69.4 1.9 collective-permute-done.11
  71.3 3.3 collective-permute-start.12
  75.4 1.2 collective-permute-done.12
  76.6 3.3 collective-permute-start.13
  79.9 0.7 fusion.40
  80.7 1.2 collective-permute-done.13
  81.9 3.3 collective-permute-start.14
  86.1 1.1 collective-permute-done.14
  88.7 5.2 %fusion.4 = f32[128,8,512]{2,1,0:T(8,128)S(1)} fusion(bf16[128,32,512]{2,1,0:T(8,128)(2,1)} %param.17, bf16[128,8,512]{2,1,0:T(8,128)(2,1)S(1)} %bitcast.62, bf16[128,32,512]{2,1,0:T(8,128)(2,1)} %param.18, f32[128,32]{1,0:T(8,128)S(1)} %fusion.24), kind=kOutput, calls=%fused_computation.9 | convolution fusion | flops 67174400 | bytes 11550720 | tf_op jit(solution)/shard_map/tkr,trs->tks/dot_general | solution.py:106
  93.9 1.6 copy.17
  95.6 1.9 fusion.29
  99.3 115.2 %all-reduce.3.cloned.1.call-done = f32[64,4096]{1,0:T(8,128)} async-done(((f32[64,4096]{1,0:T(8,128)}), f32[64,4096]{1,0:T(8,128)}) %all-reduce.3.cloned.1.call-update) | async-done | bytes 1048592
  214.4 3.1 convolution_convert_fusion
  217.5 6.8 %all-to-all-start = ((bf16[16,16,4096]{2,1,0:T(8,128)(2,1)}), bf16[16,16,4096]{2,1,0:T(8,128)(2,1)S(1)}, u32[]{:S(2)}, u32[]{:S(2)}) async-start(bf16[16,16,4096]{2,1,0:T(8,128)(2,1)} %convolution_convert_fusion), calls=%async_computation | async-start | bytes 4194304 | tf_op jit(solution)/shard_map/all_to_all | solution.py:132
  224.6 47.0 %all-to-all-done = bf16[16,16,4096]{2,1,0:T(8,128)(2,1)S(1)} async-done(((bf16[16,16,4096]{2,1,0:T(8,128)(2,1)}), bf16[16,16,4096]{2,1,0:T(8,128)(2,1)S(1)}, u32[]{:S(2)}, u32[]{:S(2)}) %all-to-all-start) | async-done | bytes 2097184 | tf_op jit(solution)/shard_map/all_to_all | solution.py:132
  272.6 6.5 %fusion.3 = f32[128,8,512]{2,1,0:T(8,128)} fusion(bf16[128,32,512]{2,1,0:T(8,128)(2,1)} %param.18, bf16[128,8,512]{2,1,0:T(8,128)(2,1)S(1)} %bitcast.61, bf16[128,32,512]{2,1,0:T(8,128)(2,1)} %param.17, f32[128,32]{1,0:T(8,128)S(1)} %fusion.24), kind=kOutput, calls=%fused_computation.8 | convolution fusion | flops 67174400 | bytes 11550720 | tf_op jit(solution)/shard_map/tkr,trc->tkc/dot_general | solution.py:142
  279.1 1.7 reshape.169
  280.8 3.8 fusion.12
  284.7 5.0 %all-to-all-start.1 = ((f32[16,16,4096]{2,1,0:T(8,128)}), f32[16,16,4096]{2,1,0:T(8,128)}, u32[]{:S(2)}, u32[]{:S(2)}) async-start(f32[16,16,4096]{2,1,0:T(8,128)} %fusion.12), calls=%async_computation.1 | async-start | bytes 8388608 | tf_op jit(solution)/shard_map/all_to_all | solution.py:149
  290.2 92.0 %all-to-all-done.1 = f32[16,16,4096]{2,1,0:T(8,128)} async-done(((f32[16,16,4096]{2,1,0:T(8,128)}), f32[16,16,4096]{2,1,0:T(8,128)}, u32[]{:S(2)}, u32[]{:S(2)}) %all-to-all-start.1) | async-done | bytes 4194336 | tf_op jit(solution)/shard_map/all_to_all | solution.py:149
  382.2 6.2 %fusion.42 = f32[16,4096,1]{1,0,2:T(8,128)S(1)} fusion(f32[16,16,16]{1,2,0:T(8,128)S(1)} %fusion.8, f32[16,16,4096]{2,1,0:T(8,128)} %all-to-all-done.1), kind=kOutput, calls=%fused_computation.109 | convolution fusion | flops 201326592 | bytes 4472832 | tf_op jit(solution)/shard_map/pqb,pqf->bf/dot_general | solution.py:150
  388.5 0.7 broadcast_multiply_fusion
  (69 shorter events, 5.8 us)
Async XLA Ops:
  6.5 207.9 %all-reduce.3.cloned.1.call-start = ((), (), s32[]{:S(2)}) async-start(), calls=%async_computation.2 | async-start | bytes 2097152
  9.3 3.8 collective-permute-start
  13.1 5.3 %collective-permute-start.1 = (bf16[16,4096]{1,0:T(8,128)(2,1)S(1)}, bf16[16,4096]{1,0:T(8,128)(2,1)S(1)}, u32[]{:S(2)}, u32[]{:S(2)}) collective-permute-start(bf16[16,4096]{1,0:T(8,128)(2,1)S(1)} %collective-permute-done), channel_id=1, source_target_pairs={{0,1},{1,2},{2,3},{3,4},{4,5},{5,6},{6,7},{7,8},{8,9},{9,10},{10,1... | collective-permute-start | bytes 393224 | tf_op jit(solution)/shard_map/ppermute | solution.py:91
  18.4 5.3 %collective-permute-start.2 = (bf16[16,4096]{1,0:T(8,128)(2,1)S(1)}, bf16[16,4096]{1,0:T(8,128)(2,1)S(1)}, u32[]{:S(2)}, u32[]{:S(2)}) collective-permute-start(bf16[16,4096]{1,0:T(8,128)(2,1)S(1)} %collective-permute-done.1), channel_id=1, source_target_pairs={{0,1},{1,2},{2,3},{3,4},{4,5},{5,6},{6,7},{7,8},{8,9},{9,10},{10,1... | collective-permute-start | bytes 393224 | tf_op jit(solution)/shard_map/ppermute | solution.py:91
  23.7 5.3 %collective-permute-start.3 = (bf16[16,4096]{1,0:T(8,128)(2,1)S(1)}, bf16[16,4096]{1,0:T(8,128)(2,1)S(1)}, u32[]{:S(2)}, u32[]{:S(2)}) collective-permute-start(bf16[16,4096]{1,0:T(8,128)(2,1)S(1)} %collective-permute-done.2), channel_id=1, source_target_pairs={{0,1},{1,2},{2,3},{3,4},{4,5},{5,6},{6,7},{7,8},{8,9},{9,10},{10,1... | collective-permute-start | bytes 393224 | tf_op jit(solution)/shard_map/ppermute | solution.py:91
  29.0 5.3 %collective-permute-start.4 = (bf16[16,4096]{1,0:T(8,128)(2,1)S(1)}, bf16[16,4096]{1,0:T(8,128)(2,1)S(1)}, u32[]{:S(2)}, u32[]{:S(2)}) collective-permute-start(bf16[16,4096]{1,0:T(8,128)(2,1)S(1)} %collective-permute-done.3), channel_id=1, source_target_pairs={{0,1},{1,2},{2,3},{3,4},{4,5},{5,6},{6,7},{7,8},{8,9},{9,10},{10,1... | collective-permute-start | bytes 393224 | tf_op jit(solution)/shard_map/ppermute | solution.py:91
  34.3 5.3 %collective-permute-start.5 = (bf16[16,4096]{1,0:T(8,128)(2,1)S(1)}, bf16[16,4096]{1,0:T(8,128)(2,1)S(1)}, u32[]{:S(2)}, u32[]{:S(2)}) collective-permute-start(bf16[16,4096]{1,0:T(8,128)(2,1)S(1)} %collective-permute-done.4), channel_id=1, source_target_pairs={{0,1},{1,2},{2,3},{3,4},{4,5},{5,6},{6,7},{7,8},{8,9},{9,10},{10,1... | collective-permute-start | bytes 393224 | tf_op jit(solution)/shard_map/ppermute | solution.py:91
  39.5 5.3 %collective-permute-start.6 = (bf16[16,4096]{1,0:T(8,128)(2,1)S(1)}, bf16[16,4096]{1,0:T(8,128)(2,1)S(1)}, u32[]{:S(2)}, u32[]{:S(2)}) collective-permute-start(bf16[16,4096]{1,0:T(8,128)(2,1)S(1)} %collective-permute-done.5), channel_id=1, source_target_pairs={{0,1},{1,2},{2,3},{3,4},{4,5},{5,6},{6,7},{7,8},{8,9},{9,10},{10,1... | collective-permute-start | bytes 393224 | tf_op jit(solution)/shard_map/ppermute | solution.py:91
  44.8 5.3 %collective-permute-start.7 = (bf16[16,4096]{1,0:T(8,128)(2,1)S(1)}, bf16[16,4096]{1,0:T(8,128)(2,1)S(1)}, u32[]{:S(2)}, u32[]{:S(2)}) collective-permute-start(bf16[16,4096]{1,0:T(8,128)(2,1)S(1)} %collective-permute-done.6), channel_id=1, source_target_pairs={{0,1},{1,2},{2,3},{3,4},{4,5},{5,6},{6,7},{7,8},{8,9},{9,10},{10,1... | collective-permute-start | bytes 393224 | tf_op jit(solution)/shard_map/ppermute | solution.py:91
  50.1 5.3 %collective-permute-start.8 = (bf16[16,4096]{1,0:T(8,128)(2,1)S(1)}, bf16[16,4096]{1,0:T(8,128)(2,1)S(1)}, u32[]{:S(2)}, u32[]{:S(2)}) collective-permute-start(bf16[16,4096]{1,0:T(8,128)(2,1)S(1)} %collective-permute-done.7), channel_id=1, source_target_pairs={{0,1},{1,2},{2,3},{3,4},{4,5},{5,6},{6,7},{7,8},{8,9},{9,10},{10,1... | collective-permute-start | bytes 393224 | tf_op jit(solution)/shard_map/ppermute | solution.py:91
  55.4 5.3 %collective-permute-start.9 = (bf16[16,4096]{1,0:T(8,128)(2,1)S(1)}, bf16[16,4096]{1,0:T(8,128)(2,1)S(1)}, u32[]{:S(2)}, u32[]{:S(2)}) collective-permute-start(bf16[16,4096]{1,0:T(8,128)(2,1)S(1)} %collective-permute-done.8), channel_id=1, source_target_pairs={{0,1},{1,2},{2,3},{3,4},{4,5},{5,6},{6,7},{7,8},{8,9},{9,10},{10,1... | collective-permute-start | bytes 393224 | tf_op jit(solution)/shard_map/ppermute | solution.py:91
  60.7 5.3 %collective-permute-start.10 = (bf16[16,4096]{1,0:T(8,128)(2,1)S(1)}, bf16[16,4096]{1,0:T(8,128)(2,1)S(1)}, u32[]{:S(2)}, u32[]{:S(2)}) collective-permute-start(bf16[16,4096]{1,0:T(8,128)(2,1)S(1)} %collective-permute-done.9), channel_id=1, source_target_pairs={{0,1},{1,2},{2,3},{3,4},{4,5},{5,6},{6,7},{7,8},{8,9},{9,10},{10,1... | collective-permute-start | bytes 393224 | tf_op jit(solution)/shard_map/ppermute | solution.py:91
  66.0 5.3 %collective-permute-start.11 = (bf16[16,4096]{1,0:T(8,128)(2,1)S(1)}, bf16[16,4096]{1,0:T(8,128)(2,1)S(1)}, u32[]{:S(2)}, u32[]{:S(2)}) collective-permute-start(bf16[16,4096]{1,0:T(8,128)(2,1)S(1)} %collective-permute-done.10), channel_id=1, source_target_pairs={{0,1},{1,2},{2,3},{3,4},{4,5},{5,6},{6,7},{7,8},{8,9},{9,10},{10,1... | collective-permute-start | bytes 393224 | tf_op jit(solution)/shard_map/ppermute | solution.py:91
  71.3 5.3 %collective-permute-start.12 = (bf16[16,4096]{1,0:T(8,128)(2,1)S(1)}, bf16[16,4096]{1,0:T(8,128)(2,1)S(1)}, u32[]{:S(2)}, u32[]{:S(2)}) collective-permute-start(bf16[16,4096]{1,0:T(8,128)(2,1)S(1)} %collective-permute-done.11), channel_id=1, source_target_pairs={{0,1},{1,2},{2,3},{3,4},{4,5},{5,6},{6,7},{7,8},{8,9},{9,10},{10,1... | collective-permute-start | bytes 393224 | tf_op jit(solution)/shard_map/ppermute | solution.py:91
  76.6 5.3 %collective-permute-start.13 = (bf16[16,4096]{1,0:T(8,128)(2,1)S(1)}, bf16[16,4096]{1,0:T(8,128)(2,1)S(1)}, u32[]{:S(2)}, u32[]{:S(2)}) collective-permute-start(bf16[16,4096]{1,0:T(8,128)(2,1)S(1)} %collective-permute-done.12), channel_id=1, source_target_pairs={{0,1},{1,2},{2,3},{3,4},{4,5},{5,6},{6,7},{7,8},{8,9},{9,10},{10,1... | collective-permute-start | bytes 393224 | tf_op jit(solution)/shard_map/ppermute | solution.py:91
  81.9 5.3 %collective-permute-start.14 = (bf16[16,4096]{1,0:T(8,128)(2,1)S(1)}, bf16[16,4096]{1,0:T(8,128)(2,1)S(1)}, u32[]{:S(2)}, u32[]{:S(2)}) collective-permute-start(bf16[16,4096]{1,0:T(8,128)(2,1)S(1)} %collective-permute-done.13), channel_id=1, source_target_pairs={{0,1},{1,2},{2,3},{3,4},{4,5},{5,6},{6,7},{7,8},{8,9},{9,10},{10,1... | collective-permute-start | bytes 393224 | tf_op jit(solution)/shard_map/ppermute | solution.py:91
  93.9 3.6 copy-start.1
  93.9 3.6 copy-start.2
  93.9 4.0 %copy-start.4 = (u32[32]{0:T(128)S(1)}, u32[32]{0:T(128)}, u32[]{:S(2)}) copy-start(u32[32]{0:T(128)} %constant.69) | copy-start | bytes 388
  93.9 5.2 %copy-start.3 = (s32[2048]{0:T(1024)S(1)}, s32[2048]{0:T(1024)}, u32[]{:S(2)}) copy-start(s32[2048]{0:T(1024)} %param.22) | copy-start | bytes 24580
  217.5 54.2 %all-to-all-start = ((bf16[16,16,4096]{2,1,0:T(8,128)(2,1)}), bf16[16,16,4096]{2,1,0:T(8,128)(2,1)S(1)}, u32[]{:S(2)}, u32[]{:S(2)}) async-start(bf16[16,16,4096]{2,1,0:T(8,128)(2,1)} %convolution_convert_fusion), calls=%async_computation | async-start | bytes 4194304 | tf_op jit(solution)/shard_map/all_to_all | solution.py:132
  284.7 5.3 %copy-start = (s32[2048]{0:T(1024)S(1)}, s32[2048]{0:T(1024)}, u32[]{:S(2)}) copy-start(s32[2048]{0:T(1024)} %param.20) | copy-start | bytes 24580
  284.7 97.5 %all-to-all-start.1 = ((f32[16,16,4096]{2,1,0:T(8,128)}), f32[16,16,4096]{2,1,0:T(8,128)}, u32[]{:S(2)}, u32[]{:S(2)}) async-start(f32[16,16,4096]{2,1,0:T(8,128)} %fusion.12), calls=%async_computation.1 | async-start | bytes 8388608 | tf_op jit(solution)/shard_map/all_to_all | solution.py:149
Sparse Core Ops, SparseCore 0:
  97.6 116.7 all-reduce.2
